TPU v7x, 32 devices: a whole 2x2x4 slice. The times are simulated.
32 devices in a mesh: group: 2 (over y), tm: 4 (over z), height: 2 (over x), width: 2 (over core).
Axes of the slice: x: 2, y: 2, z: 4, core: 2. Of those that a mesh axis runs over, the one named last changes fastest.
Arguments:
- queries: bfloat16 [8, 16, 32, 1120], P(('group', 'tm'), 'height', 'width'), parts along dimension 0, may hold values from -5 to 5
- attn_keys: bfloat16 [8, 16, 32, 1120], P(('group', 'tm'), 'height', 'width'), parts along dimension 0, may hold values from -40 to 40
- attn_values: bfloat16 [8, 16, 32, 1120], P(('group', 'tm'), 'height', 'width'), parts along dimension 0, may hold values from -7 to 7
- attn_cotangent: bfloat16 [8, 16, 32, 1120], P(('group', 'tm'), 'height', 'width'), parts along dimension 0, may hold values from -7 to 7
- clip_ids: int32 [8], P('group'), parts along dimension 0, may hold values from 0 to 1, as said below
- hidden_pre: bfloat16 [8, 16, 32, 5632], P(('group', 'tm'), 'height', 'width'), parts along dimension 0, may hold values from -6 to 6
- conv_weight: float32 [9, 5632], replicated, may hold values from -2 to 2
Outputs:
- query_grad: bfloat16 [8, 16, 32, 1120], P(('group', 'tm'), 'height', 'width'), parts along dimension 0
- key_grad: bfloat16 [8, 16, 32, 1120], P(('group', 'tm'), 'height', 'width'), parts along dimension 0
- value_gradient: bfloat16 [8, 16, 32, 1120], P(('group', 'tm'), 'height', 'width'), parts along dimension 0
- hidden_grad: bfloat16 [8, 16, 32, 5632], P(('group', 'tm'), 'height', 'width'), parts along dimension 0
There are 2 independent parts, one for each index of `group`. A program takes and returns all parts, laid end to end along the dimension named above; an argument that names none is the same for every part. Nothing has to cross between parts.
Inputs may be any that keep to these rules, and one draw needn't show every extreme that they name: clip_ids never falls; the 4 frames form two clips, 0 then 1, each of 1 to 3 frames.
All inputs are finite; a program needn't handle non-finite values.
Results may differ from a plain program's by a relative error of at most 0.001.
Values may be sent and summed in bfloat16 or wider, within the bound.
No kernel may reach another device: no remote copies, remote signals or barrier semaphores. Data moves between devices by JAX's collectives and lax.ppermute only.
A program may use at most 64 MiB of HBM per device.

v0:
```python
from functools import reduce
import jax
import jax.numpy as jnp
from jax import lax
from jax.sharding import PartitionSpec as P

HEAD_DIM = 112
HEADS = 10
EPSILON = 1e-06
TOP_PRECISION = lax.Precision.HIGHEST


def entering(value, axis, join, neutral, backward):
    count, mine = (lax.axis_size(axis), lax.axis_index(axis))
    pieces = jax.tree.map(lambda part: lax.all_gather(part, axis), value)
    if backward:
        pieces = jax.tree.map(lambda part: part[::-1], pieces)
        mine = count - 1 - mine
    so_far = jax.tree.map(
        lambda part, zero: jnp.full_like(part, 0) + jnp.asarray(zero, part.dtype), value, neutral
    )

    def turn(position, so_far):
        longer = join(so_far, jax.tree.map(lambda part: part[position], pieces))
        return jax.tree.map(lambda new, old: jnp.where(position < mine, new, old), longer, so_far)

    return lax.fori_loop(0, count - 1, turn, so_far)


def padded(block, sides, width):
    for axis, dim in sides:
        count = lax.axis_size(axis)
        forward = [(i, i + 1) for i in range(count - 1)]
        backward = [(target, source) for source, target in forward]
        low = lax.ppermute(
            lax.slice_in_dim(block, block.shape[dim] - width, None, axis=dim), axis, forward
        )
        high = lax.ppermute(lax.slice_in_dim(block, 0, width, axis=dim), axis, backward)
        block = jnp.concatenate([low, block, high], axis=dim)
    return block


def carry_on(earlier, later):
    keeping = 1.0 - later[0]
    return (
        jnp.maximum(earlier[0], later[0]),
        later[1] + keeping * earlier[1],
        later[2] + keeping * earlier[2],
    )


def clip_flags(clip_ids):
    frame = lax.axis_index("tm")
    frame_count = lax.axis_size("tm")
    current = lax.dynamic_index_in_dim(clip_ids, frame, 0, keepdims=False)
    before = lax.dynamic_index_in_dim(clip_ids, jnp.maximum(frame - 1, 0), 0, keepdims=False)
    after = lax.dynamic_index_in_dim(
        clip_ids, jnp.minimum(frame + 1, frame_count - 1), 0, keepdims=False
    )
    starts = jnp.where((frame == 0) | (current != before), 1.0, 0.0).astype(jnp.float32)
    ends = jnp.where((frame == frame_count - 1) | (current != after), 1.0, 0.0).astype(jnp.float32)
    return (starts, ends)


def glu_grad(conv_out, split_at):
    value_part = conv_out[..., :split_at]
    gate_part = conv_out[..., split_at:]
    squash = jax.nn.sigmoid(gate_part)
    glu = value_part * gate_part * squash
    value_gradient = glu * gate_part * squash
    gate_grad = glu * value_part * squash * (1.0 + gate_part * (1.0 - squash))
    return jnp.concatenate([value_gradient, gate_grad], axis=-1)


def depthwise(source, weights, start, sign, height_out, width_out):
    terms = []
    for offset_row in (-1, 0, 1):
        for offset_col in (-1, 0, 1):
            tap_index = (offset_row + 1) * 3 + offset_col + 1
            row_start = start + sign * offset_row
            col_start = start + sign * offset_col
            window = source[
                row_start : row_start + height_out, col_start : col_start + width_out
            ].astype(jnp.float32)
            terms.append(weights[tap_index] * window)
    return reduce(lambda first, second: first + second, terms)


def per_device(queries, attn_keys, attn_values, attn_cotangent, clip_ids, hidden_pre, conv_weight):
    token_count = queries.shape[1] * queries.shape[2]
    flat_width = HEADS * HEAD_DIM
    starts, ends = clip_flags(clip_ids)
    zero_flag = jnp.zeros((), jnp.float32)
    feature_keys = jnp.maximum(attn_keys, 0).reshape(token_count, HEADS, HEAD_DIM)
    value_row_block = attn_values.reshape(token_count, HEADS, HEAD_DIM)
    local_kv = jnp.einsum(
        "jrf,jrx->rfx", feature_keys, value_row_block, preferred_element_type=jnp.float32
    ).reshape(flat_width, HEAD_DIM)
    local_norm = jnp.sum(feature_keys.astype(jnp.float32), axis=0).reshape(flat_width)
    share_kv, share_norm = (
        lax.psum_scatter(local_kv, ("height", "width"), scatter_dimension=0, tiled=True),
        lax.psum_scatter(local_norm, ("height", "width"), scatter_dimension=0, tiled=True),
    )
    earlier = entering(
        (starts, share_kv, share_norm),
        "tm",
        carry_on,
        (zero_flag, jnp.zeros_like(share_kv), jnp.zeros_like(share_norm)),
        False,
    )
    part_kv = share_kv + (1.0 - starts) * earlier[1]
    part_norm = share_norm + (1.0 - starts) * earlier[2]
    state_key_value, state_norm = (
        lax.all_gather(part_kv, ("height", "width"), axis=0, tiled=True),
        lax.all_gather(part_norm, ("height", "width"), axis=0, tiled=True),
    )
    state_key_value = state_key_value.reshape(HEADS, HEAD_DIM, HEAD_DIM)
    state_norm = state_norm.reshape(HEADS, HEAD_DIM)
    feature_query = (
        jnp.maximum(queries, 0).reshape(token_count, HEADS, HEAD_DIM).astype(jnp.float32)
    )
    cotangent = attn_cotangent.reshape(token_count, HEADS, HEAD_DIM).astype(jnp.float32)
    ratio_numerator = jnp.einsum(
        "cob,obq->coq", feature_query, state_key_value, precision=TOP_PRECISION
    )
    denominator = (
        jnp.einsum("thk,hk->th", feature_query, state_norm, precision=TOP_PRECISION) + EPSILON
    )
    attended = ratio_numerator / denominator[..., None]
    scaled_gradient = cotangent / denominator[..., None]
    denominator_grad = -jnp.sum(cotangent * attended, axis=-1) / denominator
    query_feature_gradient = jnp.einsum(
        "dla,lja->dlj", scaled_gradient, state_key_value, precision=TOP_PRECISION
    )
    query_feature_gradient = query_feature_gradient + state_norm[None] * denominator_grad[..., None]
    query_grad = (
        jnp.where(feature_query > 0.0, query_feature_gradient, 0.0)
        .reshape(queries.shape)
        .astype(jnp.bfloat16)
    )
    gradient_key_value = jnp.einsum(
        "jrf,jrx->rfx", feature_query, scaled_gradient, precision=TOP_PRECISION
    ).reshape(flat_width, HEAD_DIM)
    grad_norm = jnp.einsum(
        "thk,th->hk", feature_query, denominator_grad, precision=TOP_PRECISION
    ).reshape(flat_width)
    share_grad_kv, share_grad_norm = (
        lax.psum_scatter(gradient_key_value, ("height", "width"), scatter_dimension=0, tiled=True),
        lax.psum_scatter(grad_norm, ("height", "width"), scatter_dimension=0, tiled=True),
    )
    later = entering(
        (ends, share_grad_kv, share_grad_norm),
        "tm",
        carry_on,
        (zero_flag, jnp.zeros_like(share_grad_kv), jnp.zeros_like(share_grad_norm)),
        True,
    )
    part_grad_kv = share_grad_kv + (1.0 - ends) * later[1]
    part_grad_norm = share_grad_norm + (1.0 - ends) * later[2]
    total_key_value, norm_total = (
        lax.all_gather(part_grad_kv, ("height", "width"), axis=0, tiled=True),
        lax.all_gather(part_grad_norm, ("height", "width"), axis=0, tiled=True),
    )
    total_key_value = total_key_value.reshape(HEADS, HEAD_DIM, HEAD_DIM)
    norm_total = norm_total.reshape(HEADS, HEAD_DIM)
    key_feat_grad = (
        jnp.einsum(
            "dla,lja->dlj",
            value_row_block.astype(jnp.float32),
            total_key_value,
            precision=TOP_PRECISION,
        )
        + norm_total[None]
    )
    key_grad = (
        jnp.where(feature_keys > 0, key_feat_grad, 0.0)
        .reshape(attn_keys.shape)
        .astype(jnp.bfloat16)
    )
    value_gradient = jnp.einsum(
        "cob,obq->coq", feature_keys.astype(jnp.float32), total_key_value, precision=TOP_PRECISION
    )
    value_gradient = value_gradient.reshape(attn_values.shape).astype(jnp.bfloat16)
    row_count = hidden_pre.shape[1]
    col_count = hidden_pre.shape[2]
    split_at = hidden_pre.shape[3] // 2
    widened = padded(hidden_pre, (("height", 1), ("width", 2)), 2)[0]
    conv_out = depthwise(widened, conv_weight, 1, 1, row_count + 2, col_count + 2)
    row_global = lax.axis_index("height") * row_count + jnp.arange(row_count + 2) - 1
    col_global = lax.axis_index("width") * col_count + jnp.arange(col_count + 2) - 1
    row_inside = (row_global >= 0) & (row_global < row_count * lax.axis_size("height"))
    col_inside = (col_global >= 0) & (col_global < col_count * lax.axis_size("width"))
    inside = (row_inside[:, None] & col_inside[None, :]).astype(jnp.float32)
    conv_grad = glu_grad(conv_out, split_at) * inside[:, :, None]
    hidden_grad = depthwise(conv_grad, conv_weight, 1, -1, row_count, col_count)
    hidden_grad = hidden_grad[None].astype(jnp.bfloat16)
    return (query_grad, key_grad, value_gradient, hidden_grad)


def solution(mesh):
    return jax.shard_map(
        per_device,
        mesh=mesh,
        in_specs=(
            P(("group", "tm"), "height", "width", None),
            P(("group", "tm"), "height", "width", None),
            P(("group", "tm"), "height", "width", None),
            P(("group", "tm"), "height", "width", None),
            P("group"),
            P(("group", "tm"), "height", "width", None),
            P(),
        ),
        out_specs=(
            P(("group", "tm"), "height", "width", None),
            P(("group", "tm"), "height", "width", None),
            P(("group", "tm"), "height", "width", None),
            P(("group", "tm"), "height", "width", None),
        ),
        check_vma=False,
    )
```

profile of v0, /device:TPU:0, one launch (start us, length us, event | category | flops | bytes accessed | tf_op | source)
XLA Modules:
  0.0 199.7 jit_solution(10173100332461614557)
XLA Ops:
  7.2 1.9 fusion.27
  9.1 5.7 %collective-permute-start = (bf16[1,2,16,5632]{3,2,1,0:T(8,128)(2,1)S(1)}, bf16[1,2,16,5632]{3,2,1,0:T(8,128)(2,1)}, u32[]{:S(2)}, u32[]{:S(2)}) collective-permute-start(bf16[1,2,16,5632]{3,2,1,0:T(8,128)(2,1)S(1)} %get-tuple-element.356), channel_id=1, source_target_pairs={{0,2},{1,3},{4,6},{5,7},{8,10},{9,11},{12,14},{13,15},{16,18},{17,... | collective-permute-start | bytes 1081352 | tf_op jit(solution)/shard_map/ppermute | solution.py:35
  14.8 1.4 collective-permute-start.1
  19.3 1.2 fusion.30
  21.8 8.0 %all-reduce.7 = f32[1120]{0:T(1024)S(1)} all-reduce(f32[1120]{0:T(1024)S(1)} %convert_reduce_fusion), channel_id=7, replica_groups=mesh['group'=2,'tm'=4,'height'=2,'width'=2] {'height','width'}, use_global_device_ids=true, to_apply=%region_2.3.clone | all-reduce | flops 1120 | bytes 8960
  36.7 1.5 constant_dynamic-update-slice_fusion.1
  39.2 1.2 fusion.26
  40.4 2.0 collective-permute-start.2
  42.4 1.3 collective-permute-start.3
  44.3 12.9 %all-reduce.11 = (f32[4]{0:T(128)}, f32[1120]{0:T(1024)S(1)}) all-reduce(f32[4]{0:T(128)S(1)} %dynamic-update-slice, f32[1120]{0:T(1024)S(1)} %dynamic-slice_dynamic-update-slice_fusion.1), channel_id=1, replica_groups=mesh['group'=2,'tm'=4,'height'=2,'width'=2] {'tm'}, use_global_device_ids=true, to_apply=%add | all-reduce | flops 1124 | bytes 8992
  57.9 2.4 %reshape.147 = bf16[128,10,112]{2,1,0:T(8,128)(2,1)} reshape(bf16[1,8,16,1120]{3,2,1,0:T(8,128)(2,1)} %broadcast_maximum_fusion.1) | data formatting | bytes 573440 | tf_op jit(solution)/shard_map/reshape | solution.py:120
  60.2 1.4 copy.36
  61.6 2.5 %reshape.156 = f32[128,10,112]{2,1,0:T(8,128)} reshape(bf16[1,8,16,1120]{3,2,1,0:T(8,128)(2,1)} %param.14) | data formatting | bytes 860160 | tf_op jit(solution)/shard_map/convert_element_type | solution.py:122
  64.1 2.3 %copy.39 = f32[128,10,112]{0,2,1:T(8,128)} copy(f32[128,10,112]{2,1,0:T(8,128)} %reshape.156) | data formatting | bytes 1146880 | tf_op jit(solution)/shard_map/convert_element_type | solution.py:122
  68.3 1.8 dynamic-update-slice.3
  70.8 2.4 %maximum_bitcast_fusion = bf16[12,20,5632]{2,1,0:T(8,128)(2,1)S(1)} fusion(bf16[1,12,2,5632]{3,2,1,0:T(2,128)(2,1)} %collective-permute-done.3, bf16[1,12,16,5632]{3,2,1,0:T(8,128)(2,1)S(1)} %constant_dynamic-update-slice_fusion, bf16[1,12,2,5632]{3,2,1,0:T(2,128)(2,1)} %collective-permute-done.2), kind=kLoop, calls=%fused_computation.10 | loop fusion | flops 8110080 | bytes 5406720 | tf_op jit(solution)/shard_map/squeeze | solution.py:187
  73.2 5.8 %multiply_add_fusion = f32[10,18,5632]{2,1,0:T(8,128)S(1)} fusion(bf16[12,20,5632]{2,1,0:T(8,128)(2,1)S(1)} %maximum_bitcast_fusion, f32[5632]{0:T(1024)S(1)} %get-tuple-element.317, f32[5632]{0:T(1024)S(1)} %get-tuple-element.318, f32[5632]{0:T(1024)S(1)} %get-tuple-element.311, f32[5632]{0:T(1024)S(1)} %get-tuple-element.312, ...), kind=kLoop, calls=%fused_computation.9 | loop fusion | flops 26357760 | bytes 22505472 | tf_op jit(solution)/shard_map/add | solution.py:86
  79.1 1.4 multiply_multiply_fusion
  80.5 3.0 %maximum_multiply_fusion = f32[10,18,5632]{2,1,0:T(8,128)} fusion(f32[10,18,2816]{2,1,0:T(8,128)S(1)} %get-tuple-element.352, f32[10,18,2816]{2,1,0:T(8,128)S(1)} %get-tuple-element.351, f32[10,18]{1,0:T(8,128)S(1)} %and_convert_fusion), kind=kLoop, calls=%fused_computation.8 | loop fusion | flops 2027520 | bytes 8110800 | tf_op jit(solution)/shard_map/mul | solution.py:194
  83.5 16.9 %all-gather = f32[1120,112]{1,0:T(8,128)S(1)} all-gather(f32[280,112]{1,0:T(8,128)} %reduce-scatter.7.cloned.1.call-done), channel_id=2, replica_groups=mesh['group'=2,'tm'=4,'height'=2,'width'=2] {'tm'}, dimensions={0}, use_global_device_ids=true | all-gather | bytes 627200 | tf_op jit(solution)/shard_map/all_gather | solution.py:15
  100.4 4.1 %while.32 = (s32[]{:T(128)}, f32[280,112]{1,0:T(8,128)S(1)}, f32[280]{0:T(512)S(1)}, s32[]{:T(128)}, f32[4,280,112]{2,1,0:T(8,128)S(1)}, /*index=5*/f32[4]{0:T(1...) while((s32[]{:T(128)}, f32[280,112]{1,0:T(8,128)S(1)}, f32[280]{0:T(512)S(1)}, ...), condition=%wide.region_4.5_spmd.clone, body=%wide.region_3.4_spmd.clone.sunk | while | flops 126565 | bytes 382083 | solution.py:27
  104.8 5.7 %all-reduce.2 = f32[1120]{0:T(1024)S(1)} all-reduce(f32[1120]{0:T(1024)S(1)} %add_dynamic-update-slice_fusion.1), channel_id=1, replica_groups=mesh['group'=2,'tm'=4,'height'=2,'width'=2] {'height','width'}, use_global_device_ids=true, to_apply=%add.2 | all-reduce | flops 1120 | bytes 8960
  110.9 1.6 fusion.22
  112.6 7.9 %all_gather.54 = f32[1120,112]{1,0:T(8,128)S(1)} all-gather(f32[280,112]{1,0:T(8,128)S(1)} %multiply_add_fusion.2), channel_id=1, replica_groups=mesh['group'=2,'tm'=4,'height'=2,'width'=2] {'height','width'}, dimensions={0}, use_global_device_ids=true | all-gather | bytes 627200 | tf_op jit(solution)/shard_map/all_gather | solution.py:114
  121.8 6.7 %all-reduce.9 = f32[1120]{0:T(1024)S(1)} all-reduce(f32[1120]{0:T(1024)S(1)} %reshape.154), channel_id=9, replica_groups=mesh['group'=2,'tm'=4,'height'=2,'width'=2] {'height','width'}, use_global_device_ids=true, to_apply=%region_7.8.clone | all-reduce | flops 1120 | bytes 8960
  128.6 14.8 %fusion.11 = bf16[1,8,16,5632]{3,2,1,0:T(8,128)(2,1)} fusion(f32[10,18,5632]{2,1,0:T(8,128)} %maximum_multiply_fusion, f32[5632]{0:T(1024)S(1)} %get-tuple-element.317, f32[5632]{0:T(1024)S(1)} %get-tuple-element.318, f32[5632]{0:T(1024)S(1)} %get-tuple-element.311, f32[5632]{0:T(1024)S(1)} %get-tuple-element.312, f32[5632]{0:T(1024)S(1)} %get-tuple-element.313, ...), kind=kLoop, calls=%fused_computation.33 | loop fusion | flops 12976128 | bytes 27596800 | tf_op jit(solution)/shard_map/convert_element_type | solution.py:196
  143.4 9.0 %all-reduce.10 = (f32[4]{0:T(128)S(1)}, f32[1120]{0:T(1024)S(1)}) all-reduce(f32[4]{0:T(128)S(1)} %copy-done.9, f32[1120]{0:T(1024)S(1)} %dynamic-slice_dynamic-update-slice_fusion), channel_id=1, replica_groups=mesh['group'=2,'tm'=4,'height'=2,'width'=2] {'tm'}, use_global_device_ids=true, to_apply=%add.3 | all-reduce | flops 1124 | bytes 8992
  154.0 1.1 convert_element_type.105
  155.1 15.5 %all-gather.2 = f32[1120,112]{1,0:T(8,128)S(1)} all-gather(f32[280,112]{1,0:T(8,128)} %reduce-scatter.9.cloned.1.call-done), channel_id=4, replica_groups=mesh['group'=2,'tm'=4,'height'=2,'width'=2] {'tm'}, dimensions={0}, use_global_device_ids=true | all-gather | bytes 627200 | tf_op jit(solution)/shard_map/all_gather | solution.py:15
  170.6 4.1 %while.33 = (s32[]{:T(128)}, f32[280,112]{1,0:T(8,128)S(1)}, f32[280]{0:T(512)S(1)}, s32[]{:T(128)}, f32[4,280,112]{2,1,0:T(8,128)S(1)}, /*index=5*/f32[4]{0:T(1...) while((s32[]{:T(128)}, f32[280,112]{1,0:T(8,128)S(1)}, f32[280]{0:T(512)S(1)}, ...), condition=%wide.region_9.10_spmd.clone, body=%wide.region_8.9_spmd.clone.sunk | while | flops 126565 | bytes 382083 | solution.py:27
  174.8 6.9 %all_gather.62 = f32[1120,112]{1,0:T(8,128)S(1)} all-gather(f32[280,112]{1,0:T(8,128)S(1)} %multiply_add_fusion.1), channel_id=1, replica_groups=mesh['group'=2,'tm'=4,'height'=2,'width'=2] {'height','width'}, dimensions={0}, use_global_device_ids=true | all-gather | bytes 627200 | tf_op jit(solution)/shard_map/all_gather | solution.py:161
  184.0 6.8 %all-reduce.5 = f32[1120]{0:T(1024)S(1)} all-reduce(f32[1120]{0:T(1024)S(1)} %add_dynamic-update-slice_fusion), channel_id=1, replica_groups=mesh['group'=2,'tm'=4,'height'=2,'width'=2] {'height','width'}, use_global_device_ids=true, to_apply=%add.5 | all-reduce | flops 1120 | bytes 8960
  (114 shorter events, 24.0 us)
Async XLA Ops:
  7.2 11.1 %copy-start.4 = (bf16[1,8,16,1120]{3,2,1,0:T(8,128)(2,1)S(1)}, bf16[1,8,16,1120]{3,2,1,0:T(8,128)(2,1)}, u32[]{:S(2)}) copy-start(bf16[1,8,16,1120]{3,2,1,0:T(8,128)(2,1)} %param.13) | copy-start | bytes 860164
  7.2 76.3 %reduce-scatter.7.cloned.1.call-start = ((), (), s32[]{:S(2)}) async-start(), calls=%async_computation.2 | async-start | bytes 716800
  9.1 11.5 %copy-start = (bf16[1,8,16,1120]{3,2,1,0:T(8,128)(2,1)S(1)}, bf16[1,8,16,1120]{3,2,1,0:T(8,128)(2,1)}, u32[]{:S(2)}) copy-start(bf16[1,8,16,1120]{3,2,1,0:T(8,128)(2,1)} %param.12) | copy-start | bytes 860164
  9.1 26.6 %collective-permute-start = (bf16[1,2,16,5632]{3,2,1,0:T(8,128)(2,1)S(1)}, bf16[1,2,16,5632]{3,2,1,0:T(8,128)(2,1)}, u32[]{:S(2)}, u32[]{:S(2)}) collective-permute-start(bf16[1,2,16,5632]{3,2,1,0:T(8,128)(2,1)S(1)} %get-tuple-element.356), channel_id=1, source_target_pairs={{0,2},{1,3},{4,6},{5,7},{8,10},{9,11},{12,14},{13,15},{16,18},{17,... | collective-permute-start | bytes 1081352 | tf_op jit(solution)/shard_map/ppermute | solution.py:35
  14.8 5.8 %copy-start.6 = (f32[9,5632]{1,0:T(8,128)S(1)}, f32[9,5632]{1,0:T(8,128)}, u32[]{:S(2)}) copy-start(f32[9,5632]{1,0:T(8,128)} %param.17) | copy-start | bytes 608260
  14.8 23.4 %collective-permute-start.1 = (bf16[1,2,16,5632]{3,2,1,0:T(8,128)(2,1)}, bf16[1,2,16,5632]{3,2,1,0:T(8,128)(2,1)}, u32[]{:S(2)}, u32[]{:S(2)}) collective-permute-start(bf16[1,2,16,5632]{3,2,1,0:T(8,128)(2,1)} %get-tuple-element.355), channel_id=1, source_target_pairs={{2,0},{3,1},{6,4},{7,5},{10,8},{11,9},{14,12},{15,13},{18,16},{19,... | collective-permute-start | bytes 1081352 | tf_op jit(solution)/shard_map/ppermute | solution.py:38
  17.2 12.5 %copy-start.7 = (s32[4]{0:T(128)S(1)}, s32[4]{0:T(128)}, u32[]{:S(2)}) copy-start(s32[4]{0:T(128)} %param.15) | copy-start | bytes 52
  17.3 14.5 %copy-start.11 = (u32[32]{0:T(128)S(1)}, u32[32]{0:T(128)}, u32[]{:S(2)}) copy-start(u32[32]{0:T(128)} %constant.120) | copy-start | bytes 388
  17.3 15.1 %copy-start.8 = (u32[32]{0:T(128)S(1)}, u32[32]{0:T(128)}, u32[]{:S(2)}) copy-start(u32[32]{0:T(128)} %constant.130) | copy-start | bytes 388
  17.3 17.7 %copy-start.5 = (bf16[1,8,16,1120]{3,2,1,0:T(8,128)(2,1)S(1)}, bf16[1,8,16,1120]{3,2,1,0:T(8,128)(2,1)}, u32[]{:S(2)}) copy-start(bf16[1,8,16,1120]{3,2,1,0:T(8,128)(2,1)} %param.11) | copy-start | bytes 860164
  20.5 134.6 %reduce-scatter.9.cloned.1.call-start = ((), (), s32[]{:S(2)}) async-start(), calls=%async_computation.3 | async-start | bytes 716800
  40.4 30.4 %collective-permute-start.2 = (bf16[1,12,2,5632]{3,2,1,0:T(2,128)(2,1)}, bf16[1,12,2,5632]{3,2,1,0:T(2,128)(2,1)}, u32[]{:S(2)}, u32[]{:S(2)}) collective-permute-start(bf16[1,12,2,5632]{3,2,1,0:T(2,128)(2,1)} %get-tuple-element.353), channel_id=1, source_target_pairs={{0,1},{2,3},{4,5},{6,7},{8,9},{10,11},{12,13},{14,15},{16,17},{18,... | collective-permute-start | bytes 811016 | tf_op jit(solution)/shard_map/ppermute | solution.py:35
  42.4 28.4 %collective-permute-start.3 = (bf16[1,12,2,5632]{3,2,1,0:T(2,128)(2,1)}, bf16[1,12,2,5632]{3,2,1,0:T(2,128)(2,1)}, u32[]{:S(2)}, u32[]{:S(2)}) collective-permute-start(bf16[1,12,2,5632]{3,2,1,0:T(2,128)(2,1)} %get-tuple-element.354), channel_id=1, source_target_pairs={{1,0},{3,2},{5,4},{7,6},{9,8},{11,10},{13,12},{15,14},{17,16},{19,... | collective-permute-start | bytes 811016 | tf_op jit(solution)/shard_map/ppermute | solution.py:38
  80.5 20.0 %copy-start.10 = (f32[4]{0:T(128)S(1)}, f32[4]{0:T(128)}, u32[]{:S(2)}) copy-start(f32[4]{0:T(128)} %get-tuple-element.453) | copy-start | bytes 52
  83.5 27.4 %copy-start.1 = (f32[128,10,112]{0,2,1:T(8,128)S(1)}, f32[128,10,112]{0,2,1:T(8,128)}, u32[]{:S(2)}) copy-start(f32[128,10,112]{0,2,1:T(8,128)} %copy.39) | copy-start | bytes 1720324
  100.4 12.1 %copy-start.2 = (f32[280,112]{1,0:T(8,128)S(1)}, f32[280,112]{1,0:T(8,128)}, u32[]{:S(2)}) copy-start(f32[280,112]{1,0:T(8,128)} %reduce-scatter.7.cloned.1.call-done) | copy-start | bytes 376324
  128.6 14.8 %copy-start.9 = (f32[4]{0:T(128)S(1)}, f32[4]{0:T(128)}, u32[]{:S(2)}) copy-start(f32[4]{0:T(128)} %dynamic-update-slice.3) | copy-start | bytes 52
  155.1 19.6 %copy-start.3 = (f32[280,112]{1,0:T(8,128)S(1)}, f32[280,112]{1,0:T(8,128)}, u32[]{:S(2)}) copy-start(f32[280,112]{1,0:T(8,128)} %reduce-scatter.9.cloned.1.call-done) | copy-start | bytes 376324
Sparse Core Ops, SparseCore 0:
  20.6 25.0 reduce-scatter.6
  112.7 20.6 reduce-scatter.8
where the time goes:
time: 201 us; the launch traced here: 200 us
  blocking collectives  96.2 us (48%)
  other arithmetic  32 us (16%)
  local copies, waits for them, and re-layouts  31.9 us (16%)
  between operations  18.9 us (9%)
  starting transfers between devices  10.5 us (5%)
  matrix products  6.22 us (3%)
  loops' own time  4.06 us (2%)
    unnamed x6, blocking collectives  49 us
    all_gather x2, blocking collectives, entering(): pieces = jax.tree.map(lambda part: lax.all_gather(part, axis), value)  32.4 us
    convert_element_type x1, other arithmetic, per_device(): hidden_grad = hidden_grad[None].astype(jnp.bfloat16)  14.8 us
    all_gather x1, blocking collectives, per_device(): lax.all_gather(part_kv, ('height', 'width'), axis=0, tiled=True)  7.86 us
    ppermute x2, starting transfers between devices, padded(): lax.ppermute(lax.slice_in_dim(block, block.shape[dim] - width, None, axis...  7.68 us
    unnamed x38, local copies, waits for them, and re-layouts  7.01 us
    all_gather x1, blocking collectives, per_device(): lax.all_gather(part_grad_kv, ('height', 'width'), axis=0, tiled=True)  6.9 us
    add x1, other arithmetic, depthwise(): return reduce(lambda first, second: first + second, terms)  5.8 us
  transfers between devices with their start and end apart: 6, of which 0 were waited for; matrix products, arithmetic and copies ran while one was open for 29% of the time, Pallas kernels for 0%

commit v1 on v0

--- a/solution.py
+++ b/solution.py
@@ -8,6 +8,24 @@
 HEADS = 10
 EPSILON = 1e-06
 TOP_PRECISION = lax.Precision.HIGHEST
+
+
+def collect(array, axis, dim):
+    ways, here, step = (lax.axis_size(axis), lax.axis_index(axis), array.shape[dim])
+    shape = [n * ways if d == dim else n for d, n in enumerate(array.shape)]
+    full = lax.dynamic_update_slice_in_dim(
+        jnp.zeros(shape, array.dtype), array, here * step, axis=dim
+    )
+    going_up = going_down = array
+    for far in range(1, ways // 2 + 1):
+        going_up = lax.ppermute(going_up, axis, [(d, (d + 1) % ways) for d in range(ways)])
+        full = lax.dynamic_update_slice_in_dim(full, going_up, (here - far) % ways * step, axis=dim)
+        if 2 * far < ways:
+            going_down = lax.ppermute(going_down, axis, [(d, (d - 1) % ways) for d in range(ways)])
+            full = lax.dynamic_update_slice_in_dim(
+                full, going_down, (here + far) % ways * step, axis=dim
+            )
+    return full
 
 
 def entering(value, axis, join, neutral, backward):
@@ -111,7 +129,7 @@
     part_kv = share_kv + (1.0 - starts) * earlier[1]
     part_norm = share_norm + (1.0 - starts) * earlier[2]
     state_key_value, state_norm = (
-        lax.all_gather(part_kv, ("height", "width"), axis=0, tiled=True),
+        collect(part_kv, ("height", "width"), 0),
         lax.all_gather(part_norm, ("height", "width"), axis=0, tiled=True),
     )
     state_key_value = state_key_value.reshape(HEADS, HEAD_DIM, HEAD_DIM)

time: 201 us -> 192 us (0.955)
  other arithmetic: 32 us -> 18.6 us
  waiting for transfers between devices: 0.05 us -> 4.5 us
  blocking collectives: 96.2 us -> 92.1 us
  starting transfers between devices: 10.5 us -> 14.2 us
    convert_element_type x1, other arithmetic: 14.8 us -> 3.73 us  [per_device(): hidden_grad = hidden_grad[None].astype(jnp.bfloat16)]
    all_gather x1 -> x0, blocking collectives: 7.86 us -> none  [per_device(): lax.all_gather(part_kv, ('height', 'width'), axis=0, tiled=True)]
    ppermute x0 -> x3, waiting for transfers between devices: none -> 4.46 us  [the longest x2 4.45 us: collect(): lax.ppermute(going_up, axis, [(d, (d + 1) % ways) for d in range(ways)])]
    unnamed x6, blocking collectives: 49 us -> 51.6 us
    mul x1, other arithmetic: 3.04 us -> 0.62 us  [per_device(): conv_grad = glu_grad(conv_out, split_at) * inside[:, :, None]]
    ppermute x2, starting transfers between devices: 7.68 us -> 9.73 us  [padded(): lax.ppermute(lax.slice_in_dim(block, block.shape[dim] - width, None, axis...]
    unnamed x38 -> x36, local copies, waits for them, and re-layouts: 7.01 us -> 7.31 us
  transfers between devices with their start and end apart: 6 -> 9, of which waited for: 0 -> 1; matrix products, arithmetic and copies ran while one was open for 29% -> 23% of each run, Pallas kernels for 0% -> 0%
where the time goes in v1:
time: 192 us
  blocking collectives  92.1 us (48%)
  local copies, waits for them, and re-layouts  33 us (17%)
  between operations  19.1 us (10%)
  other arithmetic  18.6 us (10%)
  starting transfers between devices  14.2 us (7%)
  matrix products  6.12 us (3%)
  waiting for transfers between devices  4.5 us (2%)
  loops' own time  4.06 us (2%)
    unnamed x6, blocking collectives  51.6 us
    all_gather x2, blocking collectives, entering(): pieces = jax.tree.map(lambda part: lax.all_gather(part, axis), value)  33.6 us
    ppermute x2, starting transfers between devices, padded(): lax.ppermute(lax.slice_in_dim(block, block.shape[dim] - width, None, axis...  9.73 us
    unnamed x36, local copies, waits for them, and re-layouts  7.31 us
    all_gather x1, blocking collectives, per_device(): lax.all_gather(part_grad_kv, ('height', 'width'), axis=0, tiled=True)  6.9 us
    add x1, other arithmetic, depthwise(): return reduce(lambda first, second: first + second, terms)  5.79 us
    convert_element_type x2, local copies, waits for them, and re-layouts, per_device(): attn_cotangent.reshape(token_count, HEADS, HEAD_DIM).astype(jnp.float32)  4.82 us
    ppermute x2, waiting for transfers between devices, collect(): lax.ppermute(going_up, axis, [(d, (d + 1) % ways) for d in range(ways)])  4.45 us
  transfers between devices with their start and end apart: 9, of which 1 were waited for; matrix products, arithmetic and copies ran while one was open for 23% of the time, Pallas kernels for 0%

profile of v1, /device:TPU:0, one launch (start us, length us, event | category | flops | bytes accessed | tf_op | source)
XLA Modules:
  0.0 191.6 jit_solution(4269447907719446334)
XLA Ops:
  9.4 1.6 reshape.149
  11.4 1.1 fusion.30
  13.4 5.6 %collective-permute-start.3 = (bf16[1,2,16,5632]{3,2,1,0:T(8,128)(2,1)S(1)}, bf16[1,2,16,5632]{3,2,1,0:T(8,128)(2,1)}, u32[]{:S(2)}, u32[]{:S(2)}) collective-permute-start(bf16[1,2,16,5632]{3,2,1,0:T(8,128)(2,1)S(1)} %get-tuple-element.358), channel_id=1, source_target_pairs={{0,2},{1,3},{4,6},{5,7},{8,10},{9,11},{12,14},{13,15},{16,18},{17,... | collective-permute-start | bytes 1081352 | tf_op jit(solution)/shard_map/ppermute | solution.py:53
  19.0 1.3 collective-permute-start.4
  20.4 10.1 %all-reduce.7 = f32[1120]{0:T(1024)S(1)} all-reduce(f32[1120]{0:T(1024)S(1)} %convert_reduce_fusion), channel_id=7, replica_groups=mesh['group'=2,'tm'=4,'height'=2,'width'=2] {'height','width'}, use_global_device_ids=true, to_apply=%region_2.3.clone | all-reduce | flops 1120 | bytes 8960
  30.5 2.3 %slice_reduce_fusion.8 = (f32[5632]{0:T(1024)S(1)}, f32[5632]{0:T(1024)S(1)}, f32[5632]{0:T(1024)S(1)}, f32[5632]{0:T(1024)S(1)}, f32[5632]{0:T(1024)S(1)}, /*in...) fusion(f32[9,5632]{1,0:T(8,128)} %param.17), kind=kLoop, calls=%fused_computation.64 | loop fusion | bytes 405504 | tf_op jit(solution)/shard_map/slice | solution.py:103
  40.6 1.5 constant_dynamic-update-slice_fusion.1
  42.1 1.2 fusion.26
  43.3 4.2 %collective-permute-start.5 = (bf16[1,12,2,5632]{3,2,1,0:T(2,128)(2,1)}, bf16[1,12,2,5632]{3,2,1,0:T(2,128)(2,1)}, u32[]{:S(2)}, u32[]{:S(2)}) collective-permute-start(bf16[1,12,2,5632]{3,2,1,0:T(2,128)(2,1)} %get-tuple-element.355), channel_id=1, source_target_pairs={{0,1},{2,3},{4,5},{6,7},{8,9},{10,11},{12,13},{14,15},{16,17},{18,... | collective-permute-start | bytes 811016 | tf_op jit(solution)/shard_map/ppermute | solution.py:53
  47.5 1.3 collective-permute-start.6
  49.3 13.1 %all-reduce.11 = (f32[4]{0:T(128)}, f32[1120]{0:T(1024)S(1)}) all-reduce(f32[4]{0:T(128)S(1)} %dynamic-update-slice, f32[1120]{0:T(1024)S(1)} %dynamic-slice_dynamic-update-slice_fusion.1), channel_id=1, replica_groups=mesh['group'=2,'tm'=4,'height'=2,'width'=2] {'tm'}, use_global_device_ids=true, to_apply=%add | all-reduce | flops 1124 | bytes 8992
  63.2 2.4 %reshape.147 = bf16[128,10,112]{2,1,0:T(8,128)(2,1)} reshape(bf16[1,8,16,1120]{3,2,1,0:T(8,128)(2,1)} %broadcast_maximum_fusion.1) | data formatting | bytes 573440 | tf_op jit(solution)/shard_map/reshape | solution.py:138
  65.6 1.4 copy.36
  67.0 2.5 %reshape.156 = f32[128,10,112]{2,1,0:T(8,128)} reshape(bf16[1,8,16,1120]{3,2,1,0:T(8,128)(2,1)} %param.14) | data formatting | bytes 860160 | tf_op jit(solution)/shard_map/convert_element_type | solution.py:140
  69.5 2.3 %copy.39 = f32[128,10,112]{0,2,1:T(8,128)} copy(f32[128,10,112]{2,1,0:T(8,128)} %reshape.156) | data formatting | bytes 1146880 | tf_op jit(solution)/shard_map/convert_element_type | solution.py:140
  73.6 1.9 dynamic-update-slice.3
  76.3 2.4 %maximum_bitcast_fusion = bf16[12,20,5632]{2,1,0:T(8,128)(2,1)S(1)} fusion(bf16[1,12,2,5632]{3,2,1,0:T(2,128)(2,1)} %collective-permute-done.6, bf16[1,12,16,5632]{3,2,1,0:T(8,128)(2,1)S(1)} %constant_dynamic-update-slice_fusion, bf16[1,12,2,5632]{3,2,1,0:T(2,128)(2,1)} %collective-permute-done.5), kind=kLoop, calls=%fused_computation.10 | loop fusion | flops 8110080 | bytes 5406720 | tf_op jit(solution)/shard_map/squeeze | solution.py:205
  78.7 5.8 %multiply_add_fusion = f32[10,18,5632]{2,1,0:T(8,128)S(1)} fusion(bf16[12,20,5632]{2,1,0:T(8,128)(2,1)S(1)} %maximum_bitcast_fusion, f32[5632]{0:T(1024)S(1)} %get-tuple-element.317, f32[5632]{0:T(1024)S(1)} %get-tuple-element.318, f32[5632]{0:T(1024)S(1)} %get-tuple-element.311, f32[5632]{0:T(1024)S(1)} %get-tuple-element.312, ...), kind=kLoop, calls=%fused_computation.9 | loop fusion | flops 26357760 | bytes 22505472 | tf_op jit(solution)/shard_map/add | solution.py:104
  84.5 1.4 multiply_multiply_fusion
  86.5 3.7 %fusion.11 = bf16[1,8,16,5632]{3,2,1,0:T(8,128)(2,1)} fusion(f32[10,18,5632]{2,1,0:T(8,128)S(1)} %maximum_multiply_fusion, f32[5632]{0:T(1024)S(1)} %get-tuple-element.317, f32[5632]{0:T(1024)S(1)} %get-tuple-element.318, f32[5632]{0:T(1024)S(1)} %get-tuple-element.311, f32[5632]{0:T(1024)S(1)} %get-tuple-element.312, f32[5632]{0:T(1024)S(1)} %get-tuple-element.313, ...), kind=kLoop, calls=%fused_computation.33 | loop fusion | flops 12976128 | bytes 27596800 | tf_op jit(solution)/shard_map/convert_element_type | solution.py:214
  90.3 16.9 %all-gather = f32[1120,112]{1,0:T(8,128)S(1)} all-gather(f32[280,112]{1,0:T(8,128)} %reduce-scatter.7.cloned.1.call-done), channel_id=2, replica_groups=mesh['group'=2,'tm'=4,'height'=2,'width'=2] {'tm'}, dimensions={0}, use_global_device_ids=true | all-gather | bytes 627200 | tf_op jit(solution)/shard_map/all_gather | solution.py:33
  107.2 4.1 %while.32 = (s32[]{:T(128)}, f32[280,112]{1,0:T(8,128)S(1)}, f32[280]{0:T(512)S(1)}, s32[]{:T(128)}, f32[4,280,112]{2,1,0:T(8,128)S(1)}, /*index=5*/f32[4]{0:T(1...) while((s32[]{:T(128)}, f32[280,112]{1,0:T(8,128)S(1)}, f32[280]{0:T(512)S(1)}, ...), condition=%wide.region_4.5_spmd.clone, body=%wide.region_3.4_spmd.clone.sunk | while | flops 126565 | bytes 382083 | solution.py:45
  111.5 1.7 collective-permute-start.1
  113.4 6.7 %all-reduce.2 = f32[1120]{0:T(1024)S(1)} all-reduce(f32[1120]{0:T(1024)S(1)} %add_dynamic-update-slice_fusion.1), channel_id=1, replica_groups=mesh['group'=2,'tm'=4,'height'=2,'width'=2] {'height','width'}, use_global_device_ids=true, to_apply=%add.2 | all-reduce | flops 1120 | bytes 8960
  120.5 1.6 fusion.22
  122.2 4.5 %collective-permute-done.2 = f32[280,112]{1,0:T(8,128)S(1)} collective-permute-done((f32[280,112]{1,0:T(8,128)S(1)}, f32[280,112]{1,0:T(8,128)S(1)}, u32[]{:S(2)}, u32[]{:S(2)}) %collective-permute-start.2) | collective-permute-done | bytes 125472 | tf_op jit(solution)/shard_map/ppermute | solution.py:21
  128.0 5.8 %all-reduce.9 = f32[1120]{0:T(1024)S(1)} all-reduce(f32[1120]{0:T(1024)S(1)} %reshape.154), channel_id=9, replica_groups=mesh['group'=2,'tm'=4,'height'=2,'width'=2] {'height','width'}, use_global_device_ids=true, to_apply=%region_7.8.clone | all-reduce | flops 1120 | bytes 8960
  134.0 9.2 %all-reduce.10 = (f32[4]{0:T(128)S(1)}, f32[1120]{0:T(1024)S(1)}) all-reduce(f32[4]{0:T(128)S(1)} %copy-done.8, f32[1120]{0:T(1024)S(1)} %dynamic-slice_dynamic-update-slice_fusion), channel_id=1, replica_groups=mesh['group'=2,'tm'=4,'height'=2,'width'=2] {'tm'}, use_global_device_ids=true, to_apply=%add.3 | all-reduce | flops 1124 | bytes 8992
  145.9 16.6 %all-gather.2 = f32[1120,112]{1,0:T(8,128)S(1)} all-gather(f32[280,112]{1,0:T(8,128)} %reduce-scatter.9.cloned.1.call-done), channel_id=4, replica_groups=mesh['group'=2,'tm'=4,'height'=2,'width'=2] {'tm'}, dimensions={0}, use_global_device_ids=true | all-gather | bytes 627200 | tf_op jit(solution)/shard_map/all_gather | solution.py:33
  162.5 4.1 %while.33 = (s32[]{:T(128)}, f32[280,112]{1,0:T(8,128)S(1)}, f32[280]{0:T(512)S(1)}, s32[]{:T(128)}, f32[4,280,112]{2,1,0:T(8,128)S(1)}, /*index=5*/f32[4]{0:T(1...) while((s32[]{:T(128)}, f32[280,112]{1,0:T(8,128)S(1)}, f32[280]{0:T(512)S(1)}, ...), condition=%wide.region_9.10_spmd.clone, body=%wide.region_8.9_spmd.clone.sunk | while | flops 126565 | bytes 382083 | solution.py:45
  166.7 6.9 %all_gather.58 = f32[1120,112]{1,0:T(8,128)S(1)} all-gather(f32[280,112]{1,0:T(8,128)S(1)} %multiply_add_fusion.1), channel_id=1, replica_groups=mesh['group'=2,'tm'=4,'height'=2,'width'=2] {'height','width'}, dimensions={0}, use_global_device_ids=true | all-gather | bytes 627200 | tf_op jit(solution)/shard_map/all_gather | solution.py:179
  175.9 6.8 %all-reduce.5 = f32[1120]{0:T(1024)S(1)} all-reduce(f32[1120]{0:T(1024)S(1)} %add_dynamic-update-slice_fusion), channel_id=1, replica_groups=mesh['group'=2,'tm'=4,'height'=2,'width'=2] {'height','width'}, use_global_device_ids=true, to_apply=%add.5 | all-reduce | flops 1120 | bytes 8960
  (121 shorter events, 24.8 us)
Async XLA Ops:
  7.2 5.4 %copy-start = (bf16[1,8,16,5632]{3,2,1,0:T(8,128)(2,1)S(1)}, bf16[1,8,16,5632]{3,2,1,0:T(8,128)(2,1)}, u32[]{:S(2)}) copy-start(bf16[1,8,16,5632]{3,2,1,0:T(8,128)(2,1)} %param.16) | copy-start | bytes 4325380
  7.2 83.1 %reduce-scatter.7.cloned.1.call-start = ((), (), s32[]{:S(2)}) async-start(), calls=%async_computation.2 | async-start | bytes 716800
  8.9 11.3 %copy-start.1 = (bf16[1,8,16,1120]{3,2,1,0:T(8,128)(2,1)S(1)}, bf16[1,8,16,1120]{3,2,1,0:T(8,128)(2,1)}, u32[]{:S(2)}) copy-start(bf16[1,8,16,1120]{3,2,1,0:T(8,128)(2,1)} %param.12) | copy-start | bytes 860164
  9.3 24.0 %copy-start.6 = (s32[4]{0:T(128)S(1)}, s32[4]{0:T(128)}, u32[]{:S(2)}) copy-start(s32[4]{0:T(128)} %param.15) | copy-start | bytes 52
  9.3 26.0 %copy-start.10 = (u32[32]{0:T(128)S(1)}, u32[32]{0:T(128)}, u32[]{:S(2)}) copy-start(u32[32]{0:T(128)} %constant.148) | copy-start | bytes 388
  9.3 26.6 %copy-start.7 = (u32[32]{0:T(128)S(1)}, u32[32]{0:T(128)}, u32[]{:S(2)}) copy-start(u32[32]{0:T(128)} %constant.158) | copy-start | bytes 388
  9.4 29.5 %copy-start.5 = (bf16[1,8,16,1120]{3,2,1,0:T(8,128)(2,1)S(1)}, bf16[1,8,16,1120]{3,2,1,0:T(8,128)(2,1)}, u32[]{:S(2)}) copy-start(bf16[1,8,16,1120]{3,2,1,0:T(8,128)(2,1)} %param.11) | copy-start | bytes 860164
  12.5 133.3 %reduce-scatter.9.cloned.1.call-start = ((), (), s32[]{:S(2)}) async-start(), calls=%async_computation.3 | async-start | bytes 716800
  13.4 26.2 %collective-permute-start.3 = (bf16[1,2,16,5632]{3,2,1,0:T(8,128)(2,1)S(1)}, bf16[1,2,16,5632]{3,2,1,0:T(8,128)(2,1)}, u32[]{:S(2)}, u32[]{:S(2)}) collective-permute-start(bf16[1,2,16,5632]{3,2,1,0:T(8,128)(2,1)S(1)} %get-tuple-element.358), channel_id=1, source_target_pairs={{0,2},{1,3},{4,6},{5,7},{8,10},{9,11},{12,14},{13,15},{16,18},{17,... | collective-permute-start | bytes 1081352 | tf_op jit(solution)/shard_map/ppermute | solution.py:53
  19.0 23.1 %collective-permute-start.4 = (bf16[1,2,16,5632]{3,2,1,0:T(8,128)(2,1)}, bf16[1,2,16,5632]{3,2,1,0:T(8,128)(2,1)S(1)}, u32[]{:S(2)}, u32[]{:S(2)}) collective-permute-start(bf16[1,2,16,5632]{3,2,1,0:T(8,128)(2,1)} %get-tuple-element.357), channel_id=1, source_target_pairs={{2,0},{3,1},{6,4},{7,5},{10,8},{11,9},{14,12},{15,13},{18,16},{19,... | collective-permute-start | bytes 1081352 | tf_op jit(solution)/shard_map/ppermute | solution.py:56
  43.3 32.9 %collective-permute-start.5 = (bf16[1,12,2,5632]{3,2,1,0:T(2,128)(2,1)}, bf16[1,12,2,5632]{3,2,1,0:T(2,128)(2,1)}, u32[]{:S(2)}, u32[]{:S(2)}) collective-permute-start(bf16[1,12,2,5632]{3,2,1,0:T(2,128)(2,1)} %get-tuple-element.355), channel_id=1, source_target_pairs={{0,1},{2,3},{4,5},{6,7},{8,9},{10,11},{12,13},{14,15},{16,17},{18,... | collective-permute-start | bytes 811016 | tf_op jit(solution)/shard_map/ppermute | solution.py:53
  47.5 28.8 %collective-permute-start.6 = (bf16[1,12,2,5632]{3,2,1,0:T(2,128)(2,1)}, bf16[1,12,2,5632]{3,2,1,0:T(2,128)(2,1)}, u32[]{:S(2)}, u32[]{:S(2)}) collective-permute-start(bf16[1,12,2,5632]{3,2,1,0:T(2,128)(2,1)} %get-tuple-element.356), channel_id=1, source_target_pairs={{1,0},{3,2},{5,4},{7,6},{9,8},{11,10},{13,12},{15,14},{17,16},{19,... | collective-permute-start | bytes 811016 | tf_op jit(solution)/shard_map/ppermute | solution.py:56
  86.5 20.7 %copy-start.9 = (f32[4]{0:T(128)S(1)}, f32[4]{0:T(128)}, u32[]{:S(2)}) copy-start(f32[4]{0:T(128)} %get-tuple-element.455) | copy-start | bytes 52
  90.3 30.2 %copy-start.2 = (f32[128,10,112]{0,2,1:T(8,128)S(1)}, f32[128,10,112]{0,2,1:T(8,128)}, u32[]{:S(2)}) copy-start(f32[128,10,112]{0,2,1:T(8,128)} %copy.39) | copy-start | bytes 1720324
  90.3 21.1 %copy-start.3 = (f32[280,112]{1,0:T(8,128)S(1)}, f32[280,112]{1,0:T(8,128)}, u32[]{:S(2)}) copy-start(f32[280,112]{1,0:T(8,128)} %reduce-scatter.7.cloned.1.call-done) | copy-start | bytes 376324
  111.4 10.6 %collective-permute-start = (f32[280,112]{1,0:T(8,128)S(1)}, f32[280,112]{1,0:T(8,128)S(1)}, u32[]{:S(2)}, u32[]{:S(2)}) collective-permute-start(f32[280,112]{1,0:T(8,128)S(1)} %get-tuple-element.352), channel_id=1, source_target_pairs={{0,1},{1,2},{2,3},{3,0},{4,5},{5,6},{6,7},{7,4},{8,9},{9,10},{10,1... | collective-permute-start | bytes 376328 | tf_op jit(solution)/shard_map/ppermute | solution.py:21
  111.5 10.7 %collective-permute-start.1 = (f32[280,112]{1,0:T(8,128)S(1)}, f32[280,112]{1,0:T(8,128)S(1)}, u32[]{:S(2)}, u32[]{:S(2)}) collective-permute-start(f32[280,112]{1,0:T(8,128)S(1)} %get-tuple-element.352), channel_id=1, source_target_pairs={{0,3},{1,0},{2,1},{3,2},{4,7},{5,4},{6,5},{7,6},{8,11},{9,8},{10,9... | collective-permute-start | bytes 376328 | tf_op jit(solution)/shard_map/ppermute | solution.py:24
  120.5 13.6 %copy-start.8 = (f32[4]{0:T(128)S(1)}, f32[4]{0:T(128)}, u32[]{:S(2)}) copy-start(f32[4]{0:T(128)} %dynamic-update-slice.3) | copy-start | bytes 52
  122.1 4.6 %collective-permute-start.2 = (f32[280,112]{1,0:T(8,128)S(1)}, f32[280,112]{1,0:T(8,128)S(1)}, u32[]{:S(2)}, u32[]{:S(2)}) collective-permute-start(f32[280,112]{1,0:T(8,128)S(1)} %collective-permute-done), channel_id=1, source_target_pairs={{0,1},{1,2},{2,3},{3,0},{4,5},{5,6},{6,7},{7,4},{8,9},{9,10},{10,1... | collective-permute-start | bytes 376328 | tf_op jit(solution)/shard_map/ppermute | solution.py:21
  145.9 20.8 %copy-start.4 = (f32[280,112]{1,0:T(8,128)S(1)}, f32[280,112]{1,0:T(8,128)}, u32[]{:S(2)}) copy-start(f32[280,112]{1,0:T(8,128)} %reduce-scatter.9.cloned.1.call-done) | copy-start | bytes 376324
Sparse Core Ops, SparseCore 0:
  12.7 24.6 reduce-scatter.6
  122.2 19.7 reduce-scatter.8
